TPU v7x, 512 devices: a whole 4x4x16 slice. The times are simulated.
512 devices in a mesh: gz: 16 (over z), xy: 32 (over x, y, core).
Axes of the slice: x: 4, y: 4, z: 16, core: 2. Of those that a mesh axis runs over, the one named last changes fastest.
Arguments:
- source: float32 [512, 128, 512], P('gz', 'xy'), may hold values from -6 to 6
- potential: float32 [512, 128, 512], P('gz', 'xy'), may hold values from -6 to 6
Outputs:
- new_potential: float32 [512, 128, 512], P('gz', 'xy')
All inputs are finite; a program needn't handle non-finite values.
Results may differ from a plain program's by a relative error of at most 0.0003.
Values sent between devices are 32-bit elements; how exact they have to be, the bound alone decides.
A program may use at most 64 MiB of HBM per device.

v0:
```python
import math
import jax
import jax.numpy as jnp
from jax import lax
from jax.sharding import PartitionSpec as P

SWEEPS = 2
SCREEN = 64
OMEGA = 0.8
HIGH = lax.Precision.HIGHEST


def with_halo(value, sides, width):
    for axis, dim in sides:
        size, length = (lax.axis_size(axis), value.shape[dim])
        up = [(i, (i + 1) % size) for i in range(size - 1)]
        down = [(j, i) for i, j in up]
        last = lax.slice_in_dim(value, length - width, length, axis=dim)
        initial = lax.slice_in_dim(value, 0, width, axis=dim)
        before = lax.ppermute(last, axis, up)
        after = lax.ppermute(initial, axis, down)
        value = jnp.concatenate([before, value, after], axis=dim)
    return value


def carried_in(value, axis, join, neutral, backward):
    count, mine = (lax.axis_size(axis), lax.axis_index(axis))
    pieces = jax.tree.map(lambda part: lax.all_gather(part, axis), value)
    if backward:
        pieces = jax.tree.map(lambda part: part[::-1], pieces)
        mine = count - 1 - mine
    total = jax.tree.map(
        lambda part, zero: jnp.full_like(part, 0) + jnp.asarray(zero, part.dtype), value, neutral
    )

    def step(position, total):
        longer = join(total, jax.tree.map(lambda part: part[position], pieces))
        return jax.tree.map(lambda new, old: jnp.where(position < mine, new, old), longer, total)

    return lax.fori_loop(0, count - 1, step, total)


def sine_table(count):
    idx = jnp.arange(1, count + 1, dtype=jnp.int32)
    turns = idx[:, None] * idx[None, :] % (2 * (count + 1))
    return math.sqrt(2.0 / (count + 1)) * jnp.sin(math.pi / (count + 1) * turns.astype(jnp.float32))


def eigenvalues(count, taken):
    idx = (jnp.arange(taken, dtype=jnp.int32) + 1).astype(jnp.float32)
    return 2.0 - 2.0 * jnp.cos(math.pi / (count + 1) * idx)


def relax(extended, rhs, kappa):
    centre = extended[1:-1, 1:-1]
    padded_y = jnp.pad(centre, ((0, 0), (0, 0), (1, 1)))
    total = extended[2:, 1:-1] + extended[:-2, 1:-1] + extended[1:-1, 2:] + extended[1:-1, :-2]
    total = total + padded_y[:, :, 2:] + padded_y[:, :, :-2]
    centre_weight = 6.0 + kappa
    return centre + OMEGA * (rhs - (centre_weight * centre - total)) / centre_weight


def smooth(field, source, kappa):
    for sweep in range(SWEEPS):
        extended = with_halo(field, (("gz", 0), ("xy", 1)), 1)
        field = relax(extended, source, kappa)
    return field


def compose(earlier, later):
    return (earlier[0] * later[0], later[0] * earlier[1] + later[1])


def solve_columns(rhs, diag):
    planes = rhs.shape[0]
    first = lax.axis_index("gz") * planes
    decay = jnp.log(0.5 * diag + jnp.sqrt(0.25 * diag * diag - 1.0))
    factor = jnp.exp(-decay)
    level = (first + jnp.arange(planes, dtype=jnp.int32)).astype(jnp.float32)
    level = level.reshape((planes,) + (1,) * diag.ndim)
    coeff = (
        factor * jnp.expm1(-2.0 * (level + 1.0) * decay) / jnp.expm1(-2.0 * (level + 2.0) * decay)
    )
    ones = jnp.ones_like(diag)
    zeros = jnp.zeros_like(diag)

    def up_step(carry, item):
        pivot, value = item
        return ((pivot * carry[0], pivot * (value + carry[1])), None)

    (lift, offset), unused = lax.scan(up_step, (ones, zeros), (coeff, rhs))
    prefix = carried_in((lift, offset), "gz", compose, (ones, zeros), False)

    def fill_up(carry, item):
        pivot, value = item
        carry = pivot * (value + carry)
        return (carry, carry)

    unused, eliminated = lax.scan(fill_up, prefix[1], (coeff, rhs))

    def down_step(carry, item):
        pivot, value = item
        return ((pivot * carry[0], value + pivot * carry[1]), None)

    (lift_top, offset_top), unused = lax.scan(
        down_step, (ones, zeros), (coeff, eliminated), reverse=True
    )
    suffix = carried_in((lift_top, offset_top), "gz", compose, (ones, zeros), True)

    def fill_down(carry, item):
        pivot, value = item
        carry = value + pivot * carry
        return (carry, carry)

    unused, solved = lax.scan(fill_down, suffix[1], (coeff, eliminated), reverse=True)
    return solved


def coarse_solve(coarse, kappa):
    planes, rows, cols = coarse.shape
    groups = lax.axis_size("xy")
    total_rows = rows * groups
    table_x = sine_table(total_rows)
    table_y = sine_table(cols)
    modes_x = eigenvalues(total_rows, total_rows)
    whole = lax.all_gather(coarse, "xy", axis=1, tiled=True)
    spec = jnp.dot(whole.reshape(-1, cols), table_y, precision=HIGH).reshape(
        planes, total_rows, cols
    )
    spec = jnp.einsum("ax,zxy->zay", table_x, spec, precision=HIGH)
    modes_y = eigenvalues(cols, cols)
    diag = 2.0 + modes_x[:, None] + modes_y[None, :] + 4.0 * kappa
    solved = solve_columns(4.0 * spec, diag)
    own_rows = lax.dynamic_slice_in_dim(table_x, lax.axis_index("xy") * rows, rows, 0)
    back = jnp.einsum("xa,zay->zxy", own_rows, solved, precision=HIGH)
    return jnp.dot(back.reshape(-1, cols), table_y, precision=HIGH).reshape(planes, rows, cols)


def body(source, potential):
    kappa = 1.0 / (SCREEN * SCREEN)
    centre_weight = 6.0 + kappa
    height, width, depth_y = source.shape
    field = smooth(potential, source, kappa)
    extended = with_halo(field, (("gz", 0), ("xy", 1)), 1)
    padded_y = jnp.pad(field, ((0, 0), (0, 0), (1, 1)))
    total = extended[2:, 1:-1] + extended[:-2, 1:-1] + extended[1:-1, 2:] + extended[1:-1, :-2]
    total = total + padded_y[:, :, 2:] + padded_y[:, :, :-2]
    residual = source - (centre_weight * field - total)
    coarse = residual.reshape(height // 2, 2, width // 2, 2, depth_y // 2, 2).mean(axis=(1, 3, 5))
    correction = coarse_solve(coarse, kappa)
    lifted = jnp.broadcast_to(
        correction[:, None, :, None, :, None], (height // 2, 2, width // 2, 2, depth_y // 2, 2)
    )
    field = field + lifted.reshape(height, width, depth_y)
    return smooth(field, source, kappa)


def solution(mesh):
    placed = (P("gz", "xy", None), P("gz", "xy", None))
    return jax.shard_map(
        body, mesh=mesh, in_specs=placed, out_specs=P("gz", "xy", None), check_vma=False
    )
```

profile of v0, /device:TPU:134, one launch (start us, length us, event | category | flops | bytes accessed | tf_op | source)
XLA Modules:
  0.0 558.7 jit_solution(7522685730354100004)
XLA Ops:
  7.3 2.0 collective-permute-start
  9.3 3.8 collective-permute-start.1
  14.2 1.9 collective-permute-done.1
  16.1 3.4 collective-permute-start.2
  19.5 1.9 collective-permute-start.3
  21.5 5.8 %collective-permute-done.3 = f32[34,1,512]{2,0,1:T(8,128)S(1)} collective-permute-done((f32[34,1,512]{2,0,1:T(8,128)S(1)}, f32[34,1,512]{2,0,1:T(8,128)S(1)}, u32[]{:S(2)}, u32[]{:S(2)}) %collective-permute-start.3) | collective-permute-done | bytes 69664 | tf_op jit(solution)/shard_map/ppermute | solution.py:20
  28.6 2.2 collective-permute-start.4
  30.8 3.6 collective-permute-start.5
  34.5 3.1 collective-permute-done.5
  37.6 1.9 collective-permute-start.6
  39.6 2.4 collective-permute-start.7
  42.0 5.4 collective-permute-done.7
  48.7 1.9 collective-permute-start.8
  50.6 3.9 collective-permute-start.9
  54.5 2.8 collective-permute-done.9
  57.4 1.9 collective-permute-start.10
  59.3 2.4 collective-permute-start.11
  61.7 5.4 collective-permute-done.11
  68.4 18.1 %reshape.130 = f32[16,2,2,2,256,2]{5,4,1,0,3,2:T(8,128)} reshape(f32[32,4,512]{2,0,1:T(8,128)S(1)} %fusion.23) | data formatting | bytes 524288 | tf_op jit(solution)/shard_map/reshape | solution.py:149
  86.5 7.0 %reduce_sum.9 = f32[16,2,256]{2,0,1:T(8,128)S(1)} reduce(f32[16,2,2,2,256,2]{5,4,1,0,3,2:T(8,128)} %reshape.130, f32[]{:T(128)} %constant.201.clone.1), dimensions={1,3,5}, to_apply=%region_0.1 | reduce | flops 57344 | bytes 294916 | tf_op jit(solution)/shard_map/reduce_sum | solution.py:149
  95.2 56.8 %all-gather.10.cloned.1.call-done = f32[16,64,256]{2,0,1:T(8,128)} async-done(((f32[16,2,256]{2,0,1:T(8,128)}), f32[16,64,256]{2,0,1:T(8,128)}) %all-gather.10.cloned.1.call-update) | async-done | bytes 1048592 | tf_op jit(solution)/shard_map/all_gather | solution.py:126
  152.0 3.8 fusion.6
  159.5 67.3 %all-gather.14.cloned.1.call-done = f32[1024,256]{1,0:T(8,128)} async-done(((f32[64,256]{1,0:T(8,128)}), f32[1024,256]{1,0:T(8,128)}) %all-gather.14.cloned.1.call-update) | async-done | bytes 1048592 | tf_op jit(solution)/shard_map/all_gather | solution.py:28
  226.8 70.0 %all-gather.12.cloned.1.call-done = f32[1024,256]{1,0:T(8,128)} async-done(((f32[64,256]{1,0:T(8,128)}), f32[1024,256]{1,0:T(8,128)}) %all-gather.12.cloned.1.call-update) | async-done | bytes 1048592 | tf_op jit(solution)/shard_map/all_gather | solution.py:28
  296.8 14.0 %while.89 = (s32[]{:T(128)}, f32[64,256]{1,0:T(8,128)S(1)}, s32[]{:T(128)}, f32[16,64,256]{2,1,0:T(8,128)}, f32[16,64,256]{2,1,0:T(8,128)}, /*index=5*/s32[]{:T(128)}, s32[]{:T(128)}) while((s32[]{:T(128)}, f32[64,256]{1,0:T(8,128)S(1)}, s32[]{:T(128)}, f32[16,64,256]{2,1,0:T(8,128)}, f32[16,64,256]{2,1,0:T(8,128)}, ...), condition=%wide.region_4.5_spmd.clone, body=%wide.region_3.4_spmd.clone.sunk | while | flops 65540 | bytes 262245 | solution.py:40
  311.7 23.3 %while.90 = (s32[]{:T(128)}, f32[64,256]{1,0:T(8,128)S(1)}, f32[64,256]{1,0:T(8,128)}, f32[16,64,256]{2,1,0:T(8,128)S(1)}, f32[16,64,256]{2,1,0:T(8,128)S(1)}, /*index=5*/s32[]{:T(128)}, s32[]{:T(128)}, s32[]{:T(128)}) while((s32[]{:T(128)}, f32[64,256]{1,0:T(8,128)S(1)}, f32[64,256]{1,0:T(8,128)}, f32[16,64,256]{2,1,0:T(8,128)S(1)}, ...), condition=%wide.region_8.9_spmd.clone, body=%wide.region_7.8_spmd.clone.sunk | while | flops 81924 | bytes 393327 | solution.py:105
  315.4 1.5 bitcast_add_fusion.6
  316.9 1.5 bitcast_add_fusion.6
  318.4 1.5 bitcast_add_fusion.6
  319.9 1.5 bitcast_add_fusion.6
  336.4 67.3 %all-gather.16.cloned.1.call-done = f32[1024,256]{1,0:T(8,128)} async-done(((f32[64,256]{1,0:T(8,128)}), f32[1024,256]{1,0:T(8,128)}) %all-gather.16.cloned.1.call-update) | async-done | bytes 1048592 | tf_op jit(solution)/shard_map/all_gather | solution.py:28
  405.0 68.6 %all-gather.18.cloned.1.call-done = f32[1024,256]{1,0:T(8,128)} async-done(((f32[64,256]{1,0:T(8,128)}), f32[1024,256]{1,0:T(8,128)}) %all-gather.18.cloned.1.call-update) | async-done | bytes 1048592 | tf_op jit(solution)/shard_map/all_gather | solution.py:28
  473.5 2.4 rev.7
  475.9 13.6 %while.91 = (s32[]{:T(128)}, f32[64,256]{1,0:T(8,128)S(1)}, s32[]{:T(128)}, f32[16,64,256]{2,1,0:T(8,128)S(1)}, f32[16,64,256]{2,1,0:T(8,128)}, /*index=5*/s32[]{:T(128)}, s32[]{:T(128)}) while((s32[]{:T(128)}, f32[64,256]{1,0:T(8,128)S(1)}, s32[]{:T(128)}, f32[16,64,256]{2,1,0:T(8,128)S(1)}, f32[16,64,256]{2,1,0:T(8,128)}, ...), condition=%wide.region_10.11_spmd.clone, body=%wide.region_9.10_spmd.clone.sunk | while | flops 65540 | bytes 262245 | solution.py:40
  492.2 6.4 %broadcast_in_dim.31 = f32[16,2,2,2,256,2]{5,4,1,0,3,2:T(8,128)} broadcast(f32[16,2,256]{2,0,1:T(8,128)S(1)} %fusion.59), dimensions={0,2,4} | broadcast | bytes 294912 | tf_op jit(solution)/shard_map/broadcast_in_dim | solution.py:151
  498.7 12.7 %reshape.131 = f32[32,4,512]{2,0,1:T(8,128)S(1)} reshape(f32[16,2,2,2,256,2]{5,4,1,0,3,2:T(8,128)} %broadcast_in_dim.31) | data formatting | bytes 524288 | tf_op jit(solution)/shard_map/reshape | solution.py:154
  511.4 4.2 collective-permute-start.12
  515.6 1.9 collective-permute-start.13
  517.6 4.8 collective-permute-done.13
  522.4 1.9 collective-permute-start.14
  524.4 2.4 collective-permute-start.15
  526.8 5.4 collective-permute-done.15
  532.5 1.9 collective-permute-start.16
  534.5 3.9 collective-permute-start.17
  538.4 2.8 collective-permute-done.17
  541.3 1.9 collective-permute-start.18
  543.2 2.4 collective-permute-start.19
  545.6 5.4 collective-permute-done.19
  (162 shorter events, 64.2 us)
Async XLA Ops:
  6.5 145.5 %all-gather.10.cloned.1.call-start = ((), (), s32[]{:S(2)}) async-start(), calls=%async_computation | async-start | bytes 1081344 | tf_op jit(solution)/shard_map/all_gather | solution.py:126
  7.3 6.9 %collective-permute-start = (f32[1,4,512]{2,0,1:T(1,128)S(1)}, f32[1,4,512]{2,0,1:T(1,128)S(1)}, u32[]{:S(2)}, u32[]{:S(2)}) collective-permute-start(f32[1,4,512]{2,0,1:T(1,128)S(1)} %copy.19), channel_id=1, source_target_pairs={{32,0},{64,32},{96,64},{128,96},{160,128},{192,160},{224,192},{256... | collective-permute-start | bytes 24584 | tf_op jit(solution)/shard_map/ppermute | solution.py:21
  9.3 6.8 %collective-permute-start.1 = (f32[1,4,512]{2,0,1:T(1,128)S(1)}, f32[1,4,512]{2,0,1:T(1,128)S(1)}, u32[]{:S(2)}, u32[]{:S(2)}) collective-permute-start(f32[1,4,512]{2,0,1:T(1,128)S(1)} %copy.21), channel_id=1, source_target_pairs={{0,32},{32,64},{64,96},{96,128},{128,160},{160,192},{192,224},{224... | collective-permute-start | bytes 24584 | tf_op jit(solution)/shard_map/ppermute | solution.py:20
  16.1 5.4 collective-permute-start.2
  19.5 7.9 %collective-permute-start.3 = (f32[34,1,512]{2,0,1:T(8,128)S(1)}, f32[34,1,512]{2,0,1:T(8,128)S(1)}, u32[]{:S(2)}, u32[]{:S(2)}) collective-permute-start(f32[34,1,512]{2,0,1:T(8,128)S(1)} %get-tuple-element.612), channel_id=1, source_target_pairs={{0,1},{1,2},{2,3},{3,4},{4,5},{5,6},{6,7},{7,8},{8,9},{9,10},{10,1... | collective-permute-start | bytes 208904 | tf_op jit(solution)/shard_map/ppermute | solution.py:20
  28.6 5.9 %collective-permute-start.4 = (f32[1,4,512]{2,0,1:T(1,128)S(1)}, f32[1,4,512]{2,0,1:T(1,128)S(1)}, u32[]{:S(2)}, u32[]{:S(2)}) collective-permute-start(f32[1,4,512]{2,0,1:T(1,128)S(1)} %get-tuple-element.620), channel_id=1, source_target_pairs={{32,0},{64,32},{96,64},{128,96},{160,128},{192,160},{224,192},{256... | collective-permute-start | bytes 24584 | tf_op jit(solution)/shard_map/ppermute | solution.py:21
  30.8 6.8 %collective-permute-start.5 = (f32[1,4,512]{2,0,1:T(1,128)S(1)}, f32[1,4,512]{2,0,1:T(1,128)S(1)}, u32[]{:S(2)}, u32[]{:S(2)}) collective-permute-start(f32[1,4,512]{2,0,1:T(1,128)S(1)} %get-tuple-element.619), channel_id=1, source_target_pairs={{0,32},{32,64},{64,96},{96,128},{128,160},{160,192},{192,224},{224... | collective-permute-start | bytes 24584 | tf_op jit(solution)/shard_map/ppermute | solution.py:20
  37.6 4.3 collective-permute-start.6
  39.6 7.9 %collective-permute-start.7 = (f32[34,1,512]{2,0,1:T(8,128)S(1)}, f32[34,1,512]{2,0,1:T(8,128)S(1)}, u32[]{:S(2)}, u32[]{:S(2)}) collective-permute-start(f32[34,1,512]{2,0,1:T(8,128)S(1)} %get-tuple-element.610), channel_id=1, source_target_pairs={{0,1},{1,2},{2,3},{3,4},{4,5},{5,6},{6,7},{7,8},{8,9},{9,10},{10,1... | collective-permute-start | bytes 208904 | tf_op jit(solution)/shard_map/ppermute | solution.py:20
  48.7 5.9 %collective-permute-start.8 = (f32[1,4,512]{2,0,1:T(1,128)S(1)}, f32[1,4,512]{2,0,1:T(1,128)S(1)}, u32[]{:S(2)}, u32[]{:S(2)}) collective-permute-start(f32[1,4,512]{2,0,1:T(1,128)S(1)} %get-tuple-element.618), channel_id=1, source_target_pairs={{32,0},{64,32},{96,64},{128,96},{160,128},{192,160},{224,192},{256... | collective-permute-start | bytes 24584 | tf_op jit(solution)/shard_map/ppermute | solution.py:21
  50.6 6.8 %collective-permute-start.9 = (f32[1,4,512]{2,0,1:T(1,128)S(1)}, f32[1,4,512]{2,0,1:T(1,128)S(1)}, u32[]{:S(2)}, u32[]{:S(2)}) collective-permute-start(f32[1,4,512]{2,0,1:T(1,128)S(1)} %get-tuple-element.617), channel_id=1, source_target_pairs={{0,32},{32,64},{64,96},{96,128},{128,160},{160,192},{192,224},{224... | collective-permute-start | bytes 24584 | tf_op jit(solution)/shard_map/ppermute | solution.py:20
  57.4 4.3 collective-permute-start.10
  59.3 7.9 %collective-permute-start.11 = (f32[34,1,512]{2,0,1:T(8,128)S(1)}, f32[34,1,512]{2,0,1:T(8,128)S(1)}, u32[]{:S(2)}, u32[]{:S(2)}) collective-permute-start(f32[34,1,512]{2,0,1:T(8,128)S(1)} %get-tuple-element.608), channel_id=1, source_target_pairs={{0,1},{1,2},{2,3},{3,4},{4,5},{5,6},{6,7},{7,8},{8,9},{9,10},{10,1... | collective-permute-start | bytes 208904 | tf_op jit(solution)/shard_map/ppermute | solution.py:20
  94.1 132.7 %all-gather.14.cloned.1.call-start = ((), (), s32[]{:S(2)}) async-start(), calls=%async_computation.2 | async-start | bytes 1114112 | tf_op jit(solution)/shard_map/all_gather | solution.py:28
  158.0 0.6 copy-start.3
  158.0 0.7 copy-start.2
  158.7 138.1 %all-gather.12.cloned.1.call-start = ((), (), s32[]{:S(2)}) async-start(), calls=%async_computation.1 | async-start | bytes 1114112 | tf_op jit(solution)/shard_map/all_gather | solution.py:28
  159.4 244.2 %all-gather.16.cloned.1.call-start = ((), (), s32[]{:S(2)}) async-start(), calls=%async_computation.3 | async-start | bytes 1114112 | tf_op jit(solution)/shard_map/all_gather | solution.py:28
  334.9 0.6 copy-start.1
  335.6 137.9 %all-gather.18.cloned.1.call-start = ((), (), s32[]{:S(2)}) async-start(), calls=%async_computation.4 | async-start | bytes 1114112 | tf_op jit(solution)/shard_map/all_gather | solution.py:28
  492.2 40.0 %copy-start = (f32[32,4,512]{2,1,0:T(4,128)S(1)}, f32[32,4,512]{2,1,0:T(4,128)}, u32[]{:S(2)}) copy-start(f32[32,4,512]{2,1,0:T(4,128)} %param.14) | copy-start | bytes 786436
  511.4 6.1 %collective-permute-start.12 = (f32[1,4,512]{2,0,1:T(1,128)S(1)}, f32[1,4,512]{2,0,1:T(1,128)S(1)}, u32[]{:S(2)}, u32[]{:S(2)}) collective-permute-start(f32[1,4,512]{2,0,1:T(1,128)S(1)} %get-tuple-element.616), channel_id=1, source_target_pairs={{32,0},{64,32},{96,64},{128,96},{160,128},{192,160},{224,192},{256... | collective-permute-start | bytes 24584 | tf_op jit(solution)/shard_map/ppermute | solution.py:21
  515.6 6.8 %collective-permute-start.13 = (f32[1,4,512]{2,0,1:T(1,128)S(1)}, f32[1,4,512]{2,0,1:T(1,128)S(1)}, u32[]{:S(2)}, u32[]{:S(2)}) collective-permute-start(f32[1,4,512]{2,0,1:T(1,128)S(1)} %get-tuple-element.615), channel_id=1, source_target_pairs={{0,32},{32,64},{64,96},{96,128},{128,160},{160,192},{192,224},{224... | collective-permute-start | bytes 24584 | tf_op jit(solution)/shard_map/ppermute | solution.py:20
  522.4 4.3 collective-permute-start.14
  524.4 7.9 %collective-permute-start.15 = (f32[34,1,512]{2,0,1:T(8,128)S(1)}, f32[34,1,512]{2,0,1:T(8,128)S(1)}, u32[]{:S(2)}, u32[]{:S(2)}) collective-permute-start(f32[34,1,512]{2,0,1:T(8,128)S(1)} %get-tuple-element.606), channel_id=1, source_target_pairs={{0,1},{1,2},{2,3},{3,4},{4,5},{5,6},{6,7},{7,8},{8,9},{9,10},{10,1... | collective-permute-start | bytes 208904 | tf_op jit(solution)/shard_map/ppermute | solution.py:20
  532.5 5.9 %collective-permute-start.16 = (f32[1,4,512]{2,0,1:T(1,128)S(1)}, f32[1,4,512]{2,0,1:T(1,128)S(1)}, u32[]{:S(2)}, u32[]{:S(2)}) collective-permute-start(f32[1,4,512]{2,0,1:T(1,128)S(1)} %get-tuple-element.614), channel_id=1, source_target_pairs={{32,0},{64,32},{96,64},{128,96},{160,128},{192,160},{224,192},{256... | collective-permute-start | bytes 24584 | tf_op jit(solution)/shard_map/ppermute | solution.py:21
  534.5 6.8 %collective-permute-start.17 = (f32[1,4,512]{2,0,1:T(1,128)S(1)}, f32[1,4,512]{2,0,1:T(1,128)S(1)}, u32[]{:S(2)}, u32[]{:S(2)}) collective-permute-start(f32[1,4,512]{2,0,1:T(1,128)S(1)} %get-tuple-element.613), channel_id=1, source_target_pairs={{0,32},{32,64},{64,96},{96,128},{128,160},{160,192},{192,224},{224... | collective-permute-start | bytes 24584 | tf_op jit(solution)/shard_map/ppermute | solution.py:20
  541.3 4.3 collective-permute-start.18
  543.2 7.9 %collective-permute-start.19 = (f32[34,1,512]{2,0,1:T(8,128)S(1)}, f32[34,1,512]{2,0,1:T(8,128)S(1)}, u32[]{:S(2)}, u32[]{:S(2)}) collective-permute-start(f32[34,1,512]{2,0,1:T(8,128)S(1)} %get-tuple-element.604), channel_id=1, source_target_pairs={{0,1},{1,2},{2,3},{3,4},{4,5},{5,6},{6,7},{7,8},{8,9},{9,10},{10,1... | collective-permute-start | bytes 208904 | tf_op jit(solution)/shard_map/ppermute | solution.py:20
Sparse Core Ops, SparseCore 0:
  94.2 57.8 all-gather.9
  158.8 67.9 all-gather.13
  228.9 67.9 all-gather.11
  335.7 67.9 all-gather.15
  405.6 67.9 all-gather.17
where the time goes:
time: 562 us; the launch traced here: 559 us
  waiting for transfers between devices  374 us (67%)
  other arithmetic  64.6 us (11%)
  starting transfers between devices  52.4 us (9%)
  local copies, waits for them, and re-layouts  45 us (8%)
  between operations  13.7 us (2%)
  matrix products  7.03 us (1%)
    all_gather x4, waiting for transfers between devices, carried_in(): pieces = jax.tree.map(lambda part: lax.all_gather(part, axis), value)  273 us
    all_gather x1, waiting for transfers between devices, coarse_solve(): whole = lax.all_gather(coarse, 'xy', axis=1, tiled=True)  56.8 us
    ppermute x10, waiting for transfers between devices, with_halo(): before = lax.ppermute(last, axis, up)  43.1 us
    ppermute x10, starting transfers between devices, with_halo(): before = lax.ppermute(last, axis, up)  28.7 us
    select_n x30, other arithmetic, step(): jnp.where(position < mine, new, old)  27 us
    ppermute x10, starting transfers between devices, with_halo(): after = lax.ppermute(initial, axis, down)  23.4 us
    add x16, other arithmetic, down_step(): return ((pivot * carry[0], value + pivot * carry[1]), None)  23.2 us
    reshape x1, local copies, waits for them, and re-layouts, body(): residual.reshape(height // 2, 2, width // 2, 2, depth_y // 2, 2)  18.1 us
  transfers between devices with their start and end apart: 25, of which 16 were waited for; matrix products, arithmetic and copies ran while one was open for 1% of the time, Pallas kernels for 0%

commit v1 on v0

--- a/solution.py
+++ b/solution.py
@@ -123,7 +123,8 @@
     table_x = sine_table(total_rows)
     table_y = sine_table(cols)
     modes_x = eigenvalues(total_rows, total_rows)
-    whole = lax.all_gather(coarse, "xy", axis=1, tiled=True)
+    stack = jnp.stack([coarse] * lax.axis_size("xy"))
+    whole = jnp.concatenate(lax.all_to_all(stack, "xy", 0, 0), axis=1)
     spec = jnp.dot(whole.reshape(-1, cols), table_y, precision=HIGH).reshape(
         planes, total_rows, cols
     )

time: 562 us -> 524 us (0.932)
  waiting for transfers between devices: 374 us -> 333 us
    all_gather x1 -> x0, waiting for transfers between devices: 56.8 us -> none  [coarse_solve(): whole = lax.all_gather(coarse, 'xy', axis=1, tiled=True)]
    all_to_all x0 -> x1, waiting for transfers between devices: none -> 14.2 us  [coarse_solve(): whole = jnp.concatenate(lax.all_to_all(stack, 'xy', 0, 0), axis=1)]
where the time goes in v1:
time: 524 us; the launch traced here: 521 us
  waiting for transfers between devices  333 us (64%)
  other arithmetic  64 us (12%)
  starting transfers between devices  57.1 us (11%)
  local copies, waits for them, and re-layouts  46.1 us (9%)
  between operations  13.7 us (3%)
  matrix products  5.81 us (1%)
    all_gather x4, waiting for transfers between devices, carried_in(): pieces = jax.tree.map(lambda part: lax.all_gather(part, axis), value)  274 us
    ppermute x10, waiting for transfers between devices, with_halo(): before = lax.ppermute(last, axis, up)  43 us
    ppermute x10, starting transfers between devices, with_halo(): before = lax.ppermute(last, axis, up)  28.7 us
    select_n x30, other arithmetic, step(): jnp.where(position < mine, new, old)  27 us
    ppermute x10, starting transfers between devices, with_halo(): after = lax.ppermute(initial, axis, down)  23.4 us
    add x16, other arithmetic, down_step(): return ((pivot * carry[0], value + pivot * carry[1]), None)  23.2 us
    reshape x1, local copies, waits for them, and re-layouts, body(): residual.reshape(height // 2, 2, width // 2, 2, depth_y // 2, 2)  18.1 us
    all_to_all x1, waiting for transfers between devices, coarse_solve(): whole = jnp.concatenate(lax.all_to_all(stack, 'xy', 0, 0), axis=1)  14.2 us
  transfers between devices with their start and end apart: 25, of which 16 were waited for; matrix products, arithmetic and copies ran while one was open for 1% of the time, Pallas kernels for 0%

profile of v1, /device:TPU:134, one launch (start us, length us, event | category | flops | bytes accessed | tf_op | source)
XLA Modules:
  0.0 521.2 jit_solution(14380890118402068433)
XLA Ops:
  7.3 2.0 collective-permute-start
  9.3 3.8 collective-permute-start.1
  14.2 1.9 collective-permute-done.1
  16.1 3.4 collective-permute-start.2
  19.5 1.9 collective-permute-start.3
  21.5 5.8 %collective-permute-done.3 = f32[34,1,512]{2,0,1:T(8,128)S(1)} collective-permute-done((f32[34,1,512]{2,0,1:T(8,128)S(1)}, f32[34,1,512]{2,0,1:T(8,128)S(1)}, u32[]{:S(2)}, u32[]{:S(2)}) %collective-permute-start.3) | collective-permute-done | bytes 69664 | tf_op jit(solution)/shard_map/ppermute | solution.py:20
  28.6 2.2 collective-permute-start.4
  30.8 3.6 collective-permute-start.5
  34.5 3.1 collective-permute-done.5
  37.6 1.9 collective-permute-start.6
  39.6 2.4 collective-permute-start.7
  42.0 5.4 %collective-permute-done.7 = f32[34,1,512]{2,0,1:T(8,128)S(1)} collective-permute-done((f32[34,1,512]{2,0,1:T(8,128)S(1)}, f32[34,1,512]{2,0,1:T(8,128)S(1)}, u32[]{:S(2)}, u32[]{:S(2)}) %collective-permute-start.7) | collective-permute-done | bytes 69664 | tf_op jit(solution)/shard_map/ppermute | solution.py:20
  48.7 1.9 collective-permute-start.8
  50.6 3.9 collective-permute-start.9
  54.5 2.8 collective-permute-done.9
  57.4 1.9 collective-permute-start.10
  59.3 2.4 collective-permute-start.11
  61.8 5.4 %collective-permute-done.11 = f32[34,1,512]{2,0,1:T(8,128)S(1)} collective-permute-done((f32[34,1,512]{2,0,1:T(8,128)S(1)}, f32[34,1,512]{2,0,1:T(8,128)S(1)}, u32[]{:S(2)}, u32[]{:S(2)}) %collective-permute-start.11) | collective-permute-done | bytes 69664 | tf_op jit(solution)/shard_map/ppermute | solution.py:20
  68.4 18.1 %reshape.134 = f32[16,2,2,2,256,2]{5,4,1,0,3,2:T(8,128)} reshape(f32[32,4,512]{2,0,1:T(8,128)S(1)} %fusion.23) | data formatting | bytes 524288 | tf_op jit(solution)/shard_map/reshape | solution.py:150
  86.5 7.0 %reduce_sum.9 = f32[16,2,256]{2,0,1:T(8,128)S(1)} reduce(f32[16,2,2,2,256,2]{5,4,1,0,3,2:T(8,128)} %reshape.134, f32[]{:T(128)} %constant.201.clone.1), dimensions={1,3,5}, to_apply=%region_0.1 | reduce | flops 57344 | bytes 294916 | tf_op jit(solution)/shard_map/reduce_sum | solution.py:150
  94.6 4.7 all-to-all-start
  100.4 14.2 %all-to-all-done = f32[32,16,2,256]{3,1,2,0:T(8,128)S(1)} async-done(((f32[32,16,2,256]{3,1,2,0:T(8,128)}), f32[32,16,2,256]{3,1,2,0:T(8,128)S(1)}, u32[]{:S(2)}, u32[]{:S(2)}) %all-to-all-start) | async-done | bytes 1048608 | tf_op jit(solution)/shard_map/all_to_all | solution.py:127
  114.6 2.5 fusion.6
  120.8 68.5 %all-gather.9.cloned.1.call-done = f32[1024,256]{1,0:T(8,128)} async-done(((f32[64,256]{1,0:T(8,128)}), f32[1024,256]{1,0:T(8,128)}) %all-gather.9.cloned.1.call-update) | async-done | bytes 1048592 | tf_op jit(solution)/shard_map/all_gather | solution.py:28
  189.3 70.0 %all-gather.11.cloned.1.call-done = f32[1024,256]{1,0:T(8,128)} async-done(((f32[64,256]{1,0:T(8,128)}), f32[1024,256]{1,0:T(8,128)}) %all-gather.11.cloned.1.call-update) | async-done | bytes 1048592 | tf_op jit(solution)/shard_map/all_gather | solution.py:28
  259.3 14.0 %while.89 = (s32[]{:T(128)}, f32[64,256]{1,0:T(8,128)S(1)}, s32[]{:T(128)}, f32[16,64,256]{2,1,0:T(8,128)}, f32[16,64,256]{2,1,0:T(8,128)}, /*index=5*/s32[]{:T(128)}, s32[]{:T(128)}) while((s32[]{:T(128)}, f32[64,256]{1,0:T(8,128)S(1)}, s32[]{:T(128)}, f32[16,64,256]{2,1,0:T(8,128)}, f32[16,64,256]{2,1,0:T(8,128)}, ...), condition=%wide.region_4.5_spmd.clone, body=%wide.region_3.4_spmd.clone.sunk | while | flops 65540 | bytes 262245 | solution.py:40
  274.1 23.3 %while.90 = (s32[]{:T(128)}, f32[64,256]{1,0:T(8,128)S(1)}, f32[64,256]{1,0:T(8,128)}, f32[16,64,256]{2,1,0:T(8,128)S(1)}, f32[16,64,256]{2,1,0:T(8,128)S(1)}, /*index=5*/s32[]{:T(128)}, s32[]{:T(128)}, s32[]{:T(128)}) while((s32[]{:T(128)}, f32[64,256]{1,0:T(8,128)S(1)}, f32[64,256]{1,0:T(8,128)}, f32[16,64,256]{2,1,0:T(8,128)S(1)}, ...), condition=%wide.region_8.9_spmd.clone, body=%wide.region_7.8_spmd.clone.sunk | while | flops 81924 | bytes 393327 | solution.py:105
  274.8 1.5 bitcast_add_fusion.6
  276.3 1.5 bitcast_add_fusion.6
  277.8 1.5 bitcast_add_fusion.6
  298.8 67.3 %all-gather.13.cloned.1.call-done = f32[1024,256]{1,0:T(8,128)} async-done(((f32[64,256]{1,0:T(8,128)}), f32[1024,256]{1,0:T(8,128)}) %all-gather.13.cloned.1.call-update) | async-done | bytes 1048592 | tf_op jit(solution)/shard_map/all_gather | solution.py:28
  367.4 68.6 %all-gather.15.cloned.1.call-done = f32[1024,256]{1,0:T(8,128)} async-done(((f32[64,256]{1,0:T(8,128)}), f32[1024,256]{1,0:T(8,128)}) %all-gather.15.cloned.1.call-update) | async-done | bytes 1048592 | tf_op jit(solution)/shard_map/all_gather | solution.py:28
  436.0 2.3 rev.7
  438.3 13.6 %while.91 = (s32[]{:T(128)}, f32[64,256]{1,0:T(8,128)S(1)}, s32[]{:T(128)}, f32[16,64,256]{2,1,0:T(8,128)S(1)}, f32[16,64,256]{2,1,0:T(8,128)}, /*index=5*/s32[]{:T(128)}, s32[]{:T(128)}) while((s32[]{:T(128)}, f32[64,256]{1,0:T(8,128)S(1)}, s32[]{:T(128)}, f32[16,64,256]{2,1,0:T(8,128)S(1)}, f32[16,64,256]{2,1,0:T(8,128)}, ...), condition=%wide.region_10.11_spmd.clone, body=%wide.region_9.10_spmd.clone.sunk | while | flops 65540 | bytes 262245 | solution.py:40
  454.7 6.4 %broadcast_in_dim.31 = f32[16,2,2,2,256,2]{5,4,1,0,3,2:T(8,128)} broadcast(f32[16,2,256]{2,0,1:T(8,128)S(1)} %fusion.59), dimensions={0,2,4} | broadcast | bytes 294912 | tf_op jit(solution)/shard_map/broadcast_in_dim | solution.py:152
  461.1 12.7 %reshape.136 = f32[32,4,512]{2,0,1:T(8,128)S(1)} reshape(f32[16,2,2,2,256,2]{5,4,1,0,3,2:T(8,128)} %broadcast_in_dim.31) | data formatting | bytes 524288 | tf_op jit(solution)/shard_map/reshape | solution.py:155
  473.9 4.2 collective-permute-start.12
  478.1 1.9 collective-permute-start.13
  480.1 4.8 collective-permute-done.13
  484.9 1.9 collective-permute-start.14
  486.8 2.4 collective-permute-start.15
  489.2 5.4 %collective-permute-done.15 = f32[34,1,512]{2,0,1:T(8,128)S(1)} collective-permute-done((f32[34,1,512]{2,0,1:T(8,128)S(1)}, f32[34,1,512]{2,0,1:T(8,128)S(1)}, u32[]{:S(2)}, u32[]{:S(2)}) %collective-permute-start.15) | collective-permute-done | bytes 69664 | tf_op jit(solution)/shard_map/ppermute | solution.py:20
  495.0 1.9 collective-permute-start.16
  496.9 3.9 collective-permute-start.17
  500.9 2.8 collective-permute-done.17
  503.7 1.9 collective-permute-start.18
  505.6 2.4 collective-permute-start.19
  508.1 5.4 %collective-permute-done.19 = f32[34,1,512]{2,0,1:T(8,128)S(1)} collective-permute-done((f32[34,1,512]{2,0,1:T(8,128)S(1)}, f32[34,1,512]{2,0,1:T(8,128)S(1)}, u32[]{:S(2)}, u32[]{:S(2)}) %collective-permute-start.19) | collective-permute-done | bytes 69664 | tf_op jit(solution)/shard_map/ppermute | solution.py:20
  (162 shorter events, 66.2 us)
Async XLA Ops:
  7.3 6.9 %collective-permute-start = (f32[1,4,512]{2,0,1:T(1,128)S(1)}, f32[1,4,512]{2,0,1:T(1,128)S(1)}, u32[]{:S(2)}, u32[]{:S(2)}) collective-permute-start(f32[1,4,512]{2,0,1:T(1,128)S(1)} %copy.5), channel_id=1, source_target_pairs={{32,0},{64,32},{96,64},{128,96},{160,128},{192,160},{224,192},{256... | collective-permute-start | bytes 24584 | tf_op jit(solution)/shard_map/ppermute | solution.py:21
  9.3 6.8 %collective-permute-start.1 = (f32[1,4,512]{2,0,1:T(1,128)S(1)}, f32[1,4,512]{2,0,1:T(1,128)S(1)}, u32[]{:S(2)}, u32[]{:S(2)}) collective-permute-start(f32[1,4,512]{2,0,1:T(1,128)S(1)} %copy.7), channel_id=1, source_target_pairs={{0,32},{32,64},{64,96},{96,128},{128,160},{160,192},{192,224},{224... | collective-permute-start | bytes 24584 | tf_op jit(solution)/shard_map/ppermute | solution.py:20
  16.1 5.4 %collective-permute-start.2 = (f32[34,1,512]{2,0,1:T(8,128)S(1)}, f32[34,1,512]{2,0,1:T(8,128)S(1)}, u32[]{:S(2)}, u32[]{:S(2)}) collective-permute-start(f32[34,1,512]{2,0,1:T(8,128)S(1)} %get-tuple-element.611), channel_id=1, source_target_pairs={{1,0},{2,1},{3,2},{4,3},{5,4},{6,5},{7,6},{8,7},{9,8},{10,9},{11,1... | collective-permute-start | bytes 208904 | tf_op jit(solution)/shard_map/ppermute | solution.py:21
  19.5 7.9 %collective-permute-start.3 = (f32[34,1,512]{2,0,1:T(8,128)S(1)}, f32[34,1,512]{2,0,1:T(8,128)S(1)}, u32[]{:S(2)}, u32[]{:S(2)}) collective-permute-start(f32[34,1,512]{2,0,1:T(8,128)S(1)} %get-tuple-element.612), channel_id=1, source_target_pairs={{0,1},{1,2},{2,3},{3,4},{4,5},{5,6},{6,7},{7,8},{8,9},{9,10},{10,1... | collective-permute-start | bytes 208904 | tf_op jit(solution)/shard_map/ppermute | solution.py:20
  28.6 5.9 %collective-permute-start.4 = (f32[1,4,512]{2,0,1:T(1,128)S(1)}, f32[1,4,512]{2,0,1:T(1,128)S(1)}, u32[]{:S(2)}, u32[]{:S(2)}) collective-permute-start(f32[1,4,512]{2,0,1:T(1,128)S(1)} %get-tuple-element.620), channel_id=1, source_target_pairs={{32,0},{64,32},{96,64},{128,96},{160,128},{192,160},{224,192},{256... | collective-permute-start | bytes 24584 | tf_op jit(solution)/shard_map/ppermute | solution.py:21
  30.8 6.8 %collective-permute-start.5 = (f32[1,4,512]{2,0,1:T(1,128)S(1)}, f32[1,4,512]{2,0,1:T(1,128)S(1)}, u32[]{:S(2)}, u32[]{:S(2)}) collective-permute-start(f32[1,4,512]{2,0,1:T(1,128)S(1)} %get-tuple-element.619), channel_id=1, source_target_pairs={{0,32},{32,64},{64,96},{96,128},{128,160},{160,192},{192,224},{224... | collective-permute-start | bytes 24584 | tf_op jit(solution)/shard_map/ppermute | solution.py:20
  37.6 4.3 collective-permute-start.6
  39.6 7.9 %collective-permute-start.7 = (f32[34,1,512]{2,0,1:T(8,128)S(1)}, f32[34,1,512]{2,0,1:T(8,128)S(1)}, u32[]{:S(2)}, u32[]{:S(2)}) collective-permute-start(f32[34,1,512]{2,0,1:T(8,128)S(1)} %get-tuple-element.610), channel_id=1, source_target_pairs={{0,1},{1,2},{2,3},{3,4},{4,5},{5,6},{6,7},{7,8},{8,9},{9,10},{10,1... | collective-permute-start | bytes 208904 | tf_op jit(solution)/shard_map/ppermute | solution.py:20
  48.7 5.9 %collective-permute-start.8 = (f32[1,4,512]{2,0,1:T(1,128)S(1)}, f32[1,4,512]{2,0,1:T(1,128)S(1)}, u32[]{:S(2)}, u32[]{:S(2)}) collective-permute-start(f32[1,4,512]{2,0,1:T(1,128)S(1)} %get-tuple-element.618), channel_id=1, source_target_pairs={{32,0},{64,32},{96,64},{128,96},{160,128},{192,160},{224,192},{256... | collective-permute-start | bytes 24584 | tf_op jit(solution)/shard_map/ppermute | solution.py:21
  50.6 6.8 %collective-permute-start.9 = (f32[1,4,512]{2,0,1:T(1,128)S(1)}, f32[1,4,512]{2,0,1:T(1,128)S(1)}, u32[]{:S(2)}, u32[]{:S(2)}) collective-permute-start(f32[1,4,512]{2,0,1:T(1,128)S(1)} %get-tuple-element.617), channel_id=1, source_target_pairs={{0,32},{32,64},{64,96},{96,128},{128,160},{160,192},{192,224},{224... | collective-permute-start | bytes 24584 | tf_op jit(solution)/shard_map/ppermute | solution.py:20
  57.4 4.4 collective-permute-start.10
  59.3 7.9 %collective-permute-start.11 = (f32[34,1,512]{2,0,1:T(8,128)S(1)}, f32[34,1,512]{2,0,1:T(8,128)S(1)}, u32[]{:S(2)}, u32[]{:S(2)}) collective-permute-start(f32[34,1,512]{2,0,1:T(8,128)S(1)} %get-tuple-element.608), channel_id=1, source_target_pairs={{0,1},{1,2},{2,3},{3,4},{4,5},{5,6},{6,7},{7,8},{8,9},{9,10},{10,1... | collective-permute-start | bytes 208904 | tf_op jit(solution)/shard_map/ppermute | solution.py:20
  94.6 20.0 %all-to-all-start = ((f32[32,16,2,256]{3,1,2,0:T(8,128)}), f32[32,16,2,256]{3,1,2,0:T(8,128)S(1)}, u32[]{:S(2)}, u32[]{:S(2)}) async-start(f32[32,16,2,256]{3,1,2,0:T(8,128)} %stack.2), calls=%async_computation | async-start | bytes 2097152 | tf_op jit(solution)/shard_map/all_to_all | solution.py:127
  99.3 90.0 %all-gather.9.cloned.1.call-start = ((), (), s32[]{:S(2)}) async-start(), calls=%async_computation.1 | async-start | bytes 1114112 | tf_op jit(solution)/shard_map/all_gather | solution.py:28
  119.3 0.6 copy-start.2
  119.3 0.7 copy-start.3
  120.0 139.3 %all-gather.11.cloned.1.call-start = ((), (), s32[]{:S(2)}) async-start(), calls=%async_computation.2 | async-start | bytes 1114112 | tf_op jit(solution)/shard_map/all_gather | solution.py:28
  120.7 245.4 %all-gather.13.cloned.1.call-start = ((), (), s32[]{:S(2)}) async-start(), calls=%async_computation.3 | async-start | bytes 1114112 | tf_op jit(solution)/shard_map/all_gather | solution.py:28
  297.4 0.6 copy-start.1
  298.0 138.0 %all-gather.15.cloned.1.call-start = ((), (), s32[]{:S(2)}) async-start(), calls=%async_computation.4 | async-start | bytes 1114112 | tf_op jit(solution)/shard_map/all_gather | solution.py:28
  454.7 40.0 %copy-start = (f32[32,4,512]{2,1,0:T(4,128)S(1)}, f32[32,4,512]{2,1,0:T(4,128)}, u32[]{:S(2)}) copy-start(f32[32,4,512]{2,1,0:T(4,128)} %param.14) | copy-start | bytes 786436
  473.9 6.1 %collective-permute-start.12 = (f32[1,4,512]{2,0,1:T(1,128)S(1)}, f32[1,4,512]{2,0,1:T(1,128)S(1)}, u32[]{:S(2)}, u32[]{:S(2)}) collective-permute-start(f32[1,4,512]{2,0,1:T(1,128)S(1)} %get-tuple-element.616), channel_id=1, source_target_pairs={{32,0},{64,32},{96,64},{128,96},{160,128},{192,160},{224,192},{256... | collective-permute-start | bytes 24584 | tf_op jit(solution)/shard_map/ppermute | solution.py:21
  478.1 6.8 %collective-permute-start.13 = (f32[1,4,512]{2,0,1:T(1,128)S(1)}, f32[1,4,512]{2,0,1:T(1,128)S(1)}, u32[]{:S(2)}, u32[]{:S(2)}) collective-permute-start(f32[1,4,512]{2,0,1:T(1,128)S(1)} %get-tuple-element.615), channel_id=1, source_target_pairs={{0,32},{32,64},{64,96},{96,128},{128,160},{160,192},{192,224},{224... | collective-permute-start | bytes 24584 | tf_op jit(solution)/shard_map/ppermute | solution.py:20
  484.9 4.3 collective-permute-start.14
  486.8 7.9 %collective-permute-start.15 = (f32[34,1,512]{2,0,1:T(8,128)S(1)}, f32[34,1,512]{2,0,1:T(8,128)S(1)}, u32[]{:S(2)}, u32[]{:S(2)}) collective-permute-start(f32[34,1,512]{2,0,1:T(8,128)S(1)} %get-tuple-element.606), channel_id=1, source_target_pairs={{0,1},{1,2},{2,3},{3,4},{4,5},{5,6},{6,7},{7,8},{8,9},{9,10},{10,1... | collective-permute-start | bytes 208904 | tf_op jit(solution)/shard_map/ppermute | solution.py:20
  495.0 5.9 %collective-permute-start.16 = (f32[1,4,512]{2,0,1:T(1,128)S(1)}, f32[1,4,512]{2,0,1:T(1,128)S(1)}, u32[]{:S(2)}, u32[]{:S(2)}) collective-permute-start(f32[1,4,512]{2,0,1:T(1,128)S(1)} %get-tuple-element.614), channel_id=1, source_target_pairs={{32,0},{64,32},{96,64},{128,96},{160,128},{192,160},{224,192},{256... | collective-permute-start | bytes 24584 | tf_op jit(solution)/shard_map/ppermute | solution.py:21
  496.9 6.8 %collective-permute-start.17 = (f32[1,4,512]{2,0,1:T(1,128)S(1)}, f32[1,4,512]{2,0,1:T(1,128)S(1)}, u32[]{:S(2)}, u32[]{:S(2)}) collective-permute-start(f32[1,4,512]{2,0,1:T(1,128)S(1)} %get-tuple-element.613), channel_id=1, source_target_pairs={{0,32},{32,64},{64,96},{96,128},{128,160},{160,192},{192,224},{224... | collective-permute-start | bytes 24584 | tf_op jit(solution)/shard_map/ppermute | solution.py:20
  503.7 4.3 collective-permute-start.18
  505.6 7.9 %collective-permute-start.19 = (f32[34,1,512]{2,0,1:T(8,128)S(1)}, f32[34,1,512]{2,0,1:T(8,128)S(1)}, u32[]{:S(2)}, u32[]{:S(2)}) collective-permute-start(f32[34,1,512]{2,0,1:T(8,128)S(1)} %get-tuple-element.604), channel_id=1, source_target_pairs={{0,1},{1,2},{2,3},{3,4},{4,5},{5,6},{6,7},{7,8},{8,9},{9,10},{10,1... | collective-permute-start | bytes 208904 | tf_op jit(solution)/shard_map/ppermute | solution.py:20
Sparse Core Ops, SparseCore 0:
  120.1 69.1 all-gather.8
  191.3 67.9 all-gather.10
  298.2 67.9 all-gather.12
  368.0 67.9 all-gather.14
